TPU v7x, 128 devices: a whole 4x4x4 slice. The times are simulated.
128 devices in a mesh: row: 16 (over z, x_lo, core), col: 8 (over y, x_hi).
Axes of the slice: x: 4 (x_hi: 2, x_lo: 2; x = x_hi * 2 + x_lo), y: 4, z: 4, core: 2. Of those that a mesh axis runs over, the one named last changes fastest.
Arguments:
- layer_input: bfloat16 [4096, 8192], P('row', 'col'), may hold values from -6 to 6
- attn_grad: bfloat16 [4096, 8192], P('row', 'col'), may hold values from -6 to 6
- queries: bfloat16 [16, 256, 8192], P('row', None, 'col'), may hold values from -6 to 6
- keys: bfloat16 [16, 256, 8192], P('row', None, 'col'), may hold values from -6 to 6
- values: bfloat16 [16, 256, 8192], P('row', None, 'col'), may hold values from -6 to 6
- masked: int32 [16, 256], P('row'), may hold values 0 or 1
- key_bias: float32 [64], P('col'), may hold values from -2 to 2
- w_query: bfloat16 [8192, 8192], P('row', 'col'), may hold values from -0.0625 to 0.0625
- w_key: bfloat16 [8192, 8192], P('row', 'col'), may hold values from -0.0625 to 0.0625
- w_value: bfloat16 [8192, 8192], P('row', 'col'), may hold values from -0.0625 to 0.0625
Outputs:
- layer_grad: bfloat16 [4096, 8192], P('row', 'col')
- w_query_grad: bfloat16 [8192, 8192], P('row', 'col')
- w_key_grad: bfloat16 [8192, 8192], P('row', 'col')
- w_value_grad: bfloat16 [8192, 8192], P('row', 'col')
- bias_grad: float32 [64], P('col')
All inputs are finite; a program needn't handle non-finite values. No bound on the sum of `masked` on one device may be relied on, other than what follows from the above.
Results may differ from a plain program's by a relative error of at most 0.015.
Values may be sent and summed in bfloat16 or wider, within the bound.
A program may use at most 192 MiB of HBM per device.

v0:
```python
import jax
import jax.numpy as jnp
from jax import lax
from jax.sharding import PartitionSpec as P


def attend_back(query_c, key_c, value_c, grad_c, flag_c, key_bias):
    length = query_c.shape[0]
    heads_local = key_bias.shape[0]
    head_dim = query_c.shape[1] // heads_local
    scale_qk = 1.0 / jnp.sqrt(jnp.float32(head_dim))
    query_h = query_c.reshape(length, heads_local, head_dim)
    key_h = key_c.reshape(length, heads_local, head_dim)
    value_h = value_c.reshape(length, heads_local, head_dim)
    grad_h = grad_c.reshape(length, heads_local, head_dim)
    flag_float = flag_c.astype(jnp.float32)
    scores = (
        jnp.einsum("ihd,jhd->hij", query_h, key_h, preferred_element_type=jnp.float32) * scale_qk
        + key_bias[:, None, None] * flag_float[None, None, :]
    )
    row_max = jnp.max(scores, axis=-1, keepdims=True)
    exp_terms = jnp.exp(scores - row_max)
    attn_probs = exp_terms / jnp.sum(exp_terms, axis=-1, keepdims=True)
    probs_low = attn_probs.astype(jnp.bfloat16)
    attended = jnp.einsum("hij,jhd->ihd", probs_low, value_h, preferred_element_type=jnp.float32)
    delta = jnp.sum(grad_h.astype(jnp.float32) * attended, axis=-1)
    grad_probs = jnp.einsum("ihd,jhd->hij", grad_h, value_h, preferred_element_type=jnp.float32)
    grad_scores = attn_probs * (grad_probs - jnp.transpose(delta)[:, :, None])
    grad_low = grad_scores.astype(jnp.bfloat16)
    value_grad = jnp.einsum(
        "hij,ihd->jhd", probs_low, grad_h, preferred_element_type=jnp.float32
    ).astype(jnp.bfloat16)
    query_grad = (
        jnp.einsum("hij,jhd->ihd", grad_low, key_h, preferred_element_type=jnp.float32) * scale_qk
    ).astype(jnp.bfloat16)
    key_grad = (
        jnp.einsum("hij,ihd->jhd", grad_low, query_h, preferred_element_type=jnp.float32) * scale_qk
    ).astype(jnp.bfloat16)
    bias_part = jnp.sum(grad_scores * flag_float[None, None, :], axis=(1, 2))
    width = query_c.shape[1]
    return (
        query_grad.reshape(length, width),
        key_grad.reshape(length, width),
        value_grad.reshape(length, width),
        bias_part,
    )


def local(layer_input, attn_grad, queries, keys, values, masked, key_bias, w_query, w_key, w_value):
    row_count = lax.axis_size("row")
    col_count = lax.axis_size("col")
    width_col = attn_grad.shape[1]
    canvases_here = queries.shape[0]
    length = queries.shape[1]
    tok_local = canvases_here * length
    rows_in = w_query.shape[0]
    spread_k = row_count // col_count
    grad_canvas = attn_grad.reshape(canvases_here, length, width_col)

    def one_canvas(inputs_one):
        return attend_back(
            inputs_one[0], inputs_one[1], inputs_one[2], inputs_one[3], inputs_one[4], key_bias
        )

    query_grad, key_grad, value_grad, bias_parts = lax.map(
        one_canvas, (queries, keys, values, grad_canvas, masked)
    )
    bias_grad = lax.psum(jnp.sum(bias_parts, axis=0), "row")
    gathered = (
        lax.all_gather(query_grad, "row", axis=0, tiled=True),
        lax.all_gather(key_grad, "row", axis=0, tiled=True),
        lax.all_gather(value_grad, "row", axis=0, tiled=True),
    )
    all_tokens = gathered[0].shape[0] * length
    flat_grads = tuple((member.reshape(all_tokens, width_col) for member in gathered))
    widened = lax.all_gather(layer_input, "col", axis=1, tiled=True)
    spread = lax.all_to_all(widened, "row", split_axis=1, concat_axis=0, tiled=True)
    weight_grads = tuple(
        (
            lax.dot_general(
                spread, member, (((0,), (0,)), ((), ())), preferred_element_type=jnp.float32
            ).astype(jnp.bfloat16)
            for member in flat_grads
        )
    )
    contract = (((1,), (1,)), ((), ()))
    partial_value = lax.dot_general(
        flat_grads[0], w_query, contract, preferred_element_type=jnp.float32
    )
    partial_value = partial_value + lax.dot_general(
        flat_grads[1], w_key, contract, preferred_element_type=jnp.float32
    )
    partial_value = partial_value + lax.dot_general(
        flat_grads[2], w_value, contract, preferred_element_type=jnp.float32
    )
    partial_low = partial_value.astype(jnp.bfloat16)
    summed = lax.psum_scatter(
        lax.optimization_barrier(partial_low).astype(jnp.float32).astype(jnp.bfloat16),
        "col",
        scatter_dimension=1,
        tiled=True,
    ).astype(jnp.float32)
    piece_width = summed.shape[1]
    sectioned = summed.astype(jnp.bfloat16).reshape(row_count, tok_local, 1, piece_width)
    arrived = lax.all_to_all(
        lax.all_to_all(sectioned, "row", split_axis=0, concat_axis=2, tiled=True),
        "col",
        split_axis=2,
        concat_axis=3,
        tiled=True,
    )
    layer_grad = arrived.reshape(tok_local, spread_k * rows_in)
    return (layer_grad, weight_grads[0], weight_grads[1], weight_grads[2], bias_grad)


def solution(mesh):
    in_specs = (
        P("row", "col"),
        P("row", "col"),
        P("row", None, "col"),
        P("row", None, "col"),
        P("row", None, "col"),
        P("row", None),
        P("col"),
        P("row", "col"),
        P("row", "col"),
        P("row", "col"),
    )
    out_specs = (P("row", "col"), P("row", "col"), P("row", "col"), P("row", "col"), P("col"))
    return jax.shard_map(local, mesh=mesh, in_specs=in_specs, out_specs=out_specs, check_vma=False)
```

profile of v0, /device:TPU:109, one launch (start us, length us, event | category | flops | bytes accessed | tf_op | source)
XLA Modules:
  0.0 423.1 jit_solution(10850841933080793586)
XLA Ops:
  7.2 0.0 copy-start
  7.2 0.0 copy-start.5
  7.2 0.0 all-gather.5.cloned.1.call-start
  7.2 0.8 convert_element_type.65
  8.0 1.2 copy.80
  9.2 0.0 copy-start.3
  9.3 1.4 copy.118
  10.7 1.2 copy.117
  11.9 1.2 copy.119
  13.2 0.0 copy-start.4
  13.2 0.0 copy-done.5
  13.2 0.1 broadcast_multiply_fusion
  13.3 2.2 fusion.37
  15.5 2.1 fusion.26
  17.6 0.0 copy-done.3
  17.6 0.0 copy-done.4
  17.6 0.1 copy-done.8
  17.7 2.0 multiply_reduce_fusion
  19.7 1.1 fusion.25
  20.8 2.0 copy.88
  22.8 0.0 all-gather.5.cloned.1.call-update
  22.9 0.0 all-gather.7.cloned.1.call-start
  22.9 0.5 fusion.24
  23.4 1.0 copy.91
  24.4 0.0 all-gather.7.cloned.1.call-update
  24.4 0.0 copy-start.2
  24.4 0.0 all-gather.9.cloned.1.call-start
  24.5 2.2 convolution_convert_fusion
  26.7 1.0 copy.93
  27.7 0.0 all-gather.9.cloned.1.call-update
  27.7 0.0 all-gather.11.cloned.1.call-start
  27.8 0.0 copy-done.2
  27.8 1.0 copy.97
  28.8 0.0 all-gather.11.cloned.1.call-update
  28.8 0.2 reduce-scatter.4.cloned.1.call-start
  29.0 47.3 %all-gather.5.cloned.1.call-done = bf16[16,256,1024]{2,1,0:T(8,128)(2,1)} async-done(((bf16[1,256,1024]{2,1,0:T(8,128)(2,1)}), bf16[16,256,1024]{2,1,0:T(8,128)(2,1)}) %all-gather.5.cloned.1.call-update) | async-done | bytes 8388624 | tf_op jit(solution)/shard_map/all_gather | solution.py:70
  76.4 0.0 copy-done
  76.4 10.3 %fusion.38 = f32[4096,512]{1,0:T(8,128)} fusion(bf16[4096,1024]{1,0:T(8,128)(2,1)} %bitcast.115, bf16[512,1024]{1,0:T(8,128)(2,1)S(1)} %copy-done), kind=kOutput, calls=%fused_computation.37 | convolution fusion | flops 4294967296 | bytes 17825792 | tf_op jit(solution)/shard_map/dot_general | solution.py:87
  86.7 45.1 %all-gather.7.cloned.1.call-done = bf16[16,256,1024]{2,1,0:T(8,128)(2,1)} async-done(((bf16[1,256,1024]{2,1,0:T(8,128)(2,1)}), bf16[16,256,1024]{2,1,0:T(8,128)(2,1)}) %all-gather.7.cloned.1.call-update) | async-done | bytes 8388624 | tf_op jit(solution)/shard_map/all_gather | solution.py:71
  131.8 10.3 %fusion.39 = f32[4096,512]{1,0:T(8,128)} fusion(bf16[4096,1024]{1,0:T(8,128)(2,1)} %bitcast.116, bf16[512,1024]{1,0:T(8,128)(2,1)S(1)} %copy-done.6), kind=kOutput, calls=%fused_computation.38 | convolution fusion | flops 4294967296 | bytes 17825792 | tf_op jit(solution)/shard_map/dot_general | solution.py:90
  142.1 45.1 %all-gather.9.cloned.1.call-done = bf16[16,256,1024]{2,1,0:T(8,128)(2,1)} async-done(((bf16[1,256,1024]{2,1,0:T(8,128)(2,1)}), bf16[16,256,1024]{2,1,0:T(8,128)(2,1)}) %all-gather.9.cloned.1.call-update) | async-done | bytes 8388624 | tf_op jit(solution)/shard_map/all_gather | solution.py:72
  187.3 12.0 %add_convert_fusion = bf16[4096,512]{1,0:T(8,128)(2,1)} fusion(f32[4096,512]{1,0:T(8,128)} %fusion.38, f32[4096,512]{1,0:T(8,128)} %fusion.39, bf16[4096,1024]{1,0:T(8,128)(2,1)} %bitcast.117, bf16[512,1024]{1,0:T(8,128)(2,1)S(1)} %copy-done.7), kind=kOutput, calls=%fused_computation.1 | convolution fusion | flops 4301258752 | bytes 30408704 | tf_op jit(solution)/shard_map/dot_general | solution.py:93
  199.3 6.4 %copy.115 = bf16[4096,512]{0,1:T(8,128)(2,1)} copy(bf16[4096,512]{1,0:T(8,128)(2,1)} %add_convert_fusion) | data formatting | bytes 8388608
  205.7 0.0 reduce-scatter.4.cloned.1.call-update
  205.8 52.5 %all-gather.11.cloned.1.call-done = bf16[256,8192]{0,1:T(8,128)(2,1)} async-done(((bf16[256,1024]{0,1:T(8,128)(2,1)}), bf16[256,8192]{0,1:T(8,128)(2,1)}) %all-gather.11.cloned.1.call-update) | async-done | bytes 4194320 | tf_op jit(solution)/shard_map/all_gather | solution.py:76
  258.2 6.4 %copy.98 = bf16[256,16,512]{2,0,1:T(8,128)(2,1)} copy(bf16[256,16,512]{0,2,1:T(8,128)(2,1)} %bitcast.97) | data formatting | bytes 8388608 | tf_op jit(solution)/shard_map/all_to_all | solution.py:77
  264.7 7.0 %all-to-all-start.2 = ((bf16[256,16,512]{2,0,1:T(8,128)(2,1)}), bf16[256,16,512]{2,0,1:T(8,128)(2,1)}, u32[]{:S(2)}, u32[]{:S(2)}) async-start(bf16[256,16,512]{2,0,1:T(8,128)(2,1)} %copy.98), calls=%async_computation.2 | async-start | bytes 8388608 | tf_op jit(solution)/shard_map/all_to_all | solution.py:77
  271.6 88.1 %psum.7 = f32[8]{0:T(128)} all-reduce(f32[8]{0:T(128)S(1)} %get-tuple-element.60), channel_id=1, replica_groups=mesh['row'=16,'col'=8] {'row'}, use_global_device_ids=true, to_apply=%region_5.6 | all-reduce | flops 8 | bytes 64 | tf_op jit(solution)/shard_map/psum | solution.py:68
  359.7 0.0 all-to-all-done.2
  359.7 9.2 %fusion.14 = bf16[512,1024]{0,1:T(8,128)(2,1)S(1)} fusion(bf16[16,256,1024]{2,1,0:T(8,128)(2,1)} %all-gather.5.cloned.1.call-done, bf16[256,16,512]{2,0,1:T(8,128)(2,1)} %all-to-all-done.2), kind=kOutput, calls=%fused_computation.16 | convolution fusion | flops 4295491584 | bytes 13631488 | tf_op jit(solution)/shard_map/dot_general | solution.py:80
  368.9 0.7 reduce-scatter.4.cloned.1.call-done
  369.6 1.5 copy.116
  371.1 1.1 copy.94
  372.3 10.7 %all-to-all-start = ((bf16[16,256,1,64]{1,3,2,0:T(8,128)(2,1)}), bf16[16,256,1,64]{1,3,2,0:T(8,128)(2,1)}, u32[]{:S(2)}, u32[]{:S(2)}) async-start(bf16[16,256,1,64]{1,3,2,0:T(8,128)(2,1)} %copy.94), calls=%async_computation | async-start | bytes 1048576 | tf_op jit(solution)/shard_map/all_to_all | solution.py:106
  383.0 10.1 %fusion.17 = bf16[512,1024]{0,1:T(8,128)(2,1)} fusion(bf16[16,256,1024]{2,1,0:T(8,128)(2,1)} %all-gather.7.cloned.1.call-done, bf16[256,16,512]{2,0,1:T(8,128)(2,1)} %all-to-all-done.2), kind=kOutput, calls=%fused_computation.17 | convolution fusion | flops 4295491584 | bytes 13631488 | tf_op jit(solution)/shard_map/dot_general | solution.py:80
  393.1 0.0 all-to-all-done
  393.1 6.4 %all-to-all-start.1 = ((bf16[1,256,16,64]{1,3,0,2:T(8,128)(2,1)}), bf16[1,256,16,64]{1,3,0,2:T(8,128)(2,1)S(1)}, u32[]{:S(2)}, u32[]{:S(2)}) async-start(bf16[1,256,16,64]{1,3,0,2:T(8,128)(2,1)} %bitcast.17), calls=%async_computation.1 | async-start | bytes 1048576 | tf_op jit(solution)/shard_map/all_to_all | solution.py:105
  399.5 10.1 %fusion.20 = bf16[512,1024]{0,1:T(8,128)(2,1)} fusion(bf16[16,256,1024]{2,1,0:T(8,128)(2,1)} %all-gather.9.cloned.1.call-done, bf16[256,16,512]{2,0,1:T(8,128)(2,1)} %all-to-all-done.2), kind=kOutput, calls=%fused_computation.18 | convolution fusion | flops 4295491584 | bytes 13631488 | tf_op jit(solution)/shard_map/dot_general | solution.py:80
  409.7 1.3 copy.103
  411.0 2.3 copy.105
  413.2 2.3 copy.104
  415.5 0.0 all-to-all-done.1
  415.5 1.0 copy.102
  416.5 0.0 copy-done.1
  (7 shorter events, 0.1 us)
Async XLA Ops:
  7.2 69.2 %copy-start = (bf16[512,1024]{1,0:T(8,128)(2,1)S(1)}, bf16[512,1024]{1,0:T(8,128)(2,1)}, u32[]{:S(2)}) copy-start(bf16[512,1024]{1,0:T(8,128)(2,1)} %param.17) | copy-start | bytes 3145732
  7.2 6.0 %copy-start.5 = (f32[8]{0:T(128)S(1)}, f32[8]{0:T(128)}, u32[]{:S(2)}) copy-start(f32[8]{0:T(128)} %param.16) | copy-start | bytes 100
  7.2 69.2 %all-gather.5.cloned.1.call-start = ((), (), s32[]{:S(2)}) async-start(), calls=%async_computation.4 | async-start | bytes 8912896 | tf_op jit(solution)/shard_map/all_gather | solution.py:70
  9.2 8.3 %copy-start.3 = (bf16[256,1024]{0,1:T(8,128)(2,1)}, bf16[256,1024]{0,1:T(8,128)(2,1)S(1)}, u32[]{:S(2)}) copy-start(bf16[256,1024]{0,1:T(8,128)(2,1)S(1)} %copy.80) | copy-start | bytes 1572868
  13.2 4.4 %copy-start.4 = (bf16[1,256,1024]{1,2,0:T(8,128)(2,1)}, bf16[1,256,1024]{1,2,0:T(8,128)(2,1)S(1)}, u32[]{:S(2)}) copy-start(bf16[1,256,1024]{1,2,0:T(8,128)(2,1)S(1)} %copy.119) | copy-start | bytes 1572868
  15.5 2.2 copy-start.8
  22.9 109.0 %all-gather.7.cloned.1.call-start = ((), (), s32[]{:S(2)}) async-start(), calls=%async_computation.5 | async-start | bytes 8912896 | tf_op jit(solution)/shard_map/all_gather | solution.py:71
  24.4 3.4 copy-start.2
  24.4 162.8 %all-gather.9.cloned.1.call-start = ((), (), s32[]{:S(2)}) async-start(), calls=%async_computation.6 | async-start | bytes 8912896 | tf_op jit(solution)/shard_map/all_gather | solution.py:72
  27.7 230.5 %all-gather.11.cloned.1.call-start = ((), (), s32[]{:S(2)}) async-start(), calls=%async_computation.7 | async-start | bytes 4718592 | tf_op jit(solution)/shard_map/all_gather | solution.py:76
  28.8 340.8 %reduce-scatter.4.cloned.1.call-start = ((), (), s32[]{:S(2)}) async-start(), calls=%async_computation.8 | async-start | bytes 4718592
  76.4 55.4 %copy-start.6 = (bf16[512,1024]{1,0:T(8,128)(2,1)S(1)}, bf16[512,1024]{1,0:T(8,128)(2,1)}, u32[]{:S(2)}) copy-start(bf16[512,1024]{1,0:T(8,128)(2,1)} %param.18) | copy-start | bytes 3145732
  131.8 55.5 %copy-start.7 = (bf16[512,1024]{1,0:T(8,128)(2,1)S(1)}, bf16[512,1024]{1,0:T(8,128)(2,1)}, u32[]{:S(2)}) copy-start(bf16[512,1024]{1,0:T(8,128)(2,1)} %param.19) | copy-start | bytes 3145732
  264.7 95.0 %all-to-all-start.2 = ((bf16[256,16,512]{2,0,1:T(8,128)(2,1)}), bf16[256,16,512]{2,0,1:T(8,128)(2,1)}, u32[]{:S(2)}, u32[]{:S(2)}) async-start(bf16[256,16,512]{2,0,1:T(8,128)(2,1)} %copy.98), calls=%async_computation.2 | async-start | bytes 8388608 | tf_op jit(solution)/shard_map/all_to_all | solution.py:77
  372.3 20.8 %all-to-all-start = ((bf16[16,256,1,64]{1,3,2,0:T(8,128)(2,1)}), bf16[16,256,1,64]{1,3,2,0:T(8,128)(2,1)}, u32[]{:S(2)}, u32[]{:S(2)}) async-start(bf16[16,256,1,64]{1,3,2,0:T(8,128)(2,1)} %copy.94), calls=%async_computation | async-start | bytes 1048576 | tf_op jit(solution)/shard_map/all_to_all | solution.py:106
  393.1 22.4 %all-to-all-start.1 = ((bf16[1,256,16,64]{1,3,0,2:T(8,128)(2,1)}), bf16[1,256,16,64]{1,3,0,2:T(8,128)(2,1)S(1)}, u32[]{:S(2)}, u32[]{:S(2)}) async-start(bf16[1,256,16,64]{1,3,0,2:T(8,128)(2,1)} %bitcast.17), calls=%async_computation.1 | async-start | bytes 1048576 | tf_op jit(solution)/shard_map/all_to_all | solution.py:105
  399.5 17.0 %copy-start.1 = (bf16[512,1024]{1,0:T(8,128)(2,1)S(1)}, bf16[512,1024]{1,0:T(8,128)(2,1)}, u32[]{:S(2)}) copy-start(bf16[512,1024]{1,0:T(8,128)(2,1)} %param.17) | copy-start | bytes 3145732
Sparse Core Ops, SparseCore 0:
  23.0 53.3 all-gather.4
  78.6 53.1 all-gather.6
  134.1 53.1 all-gather.8
  190.0 68.1 all-gather.10
  261.9 107.6 reduce-scatter.3
where the time goes:
time: 426 us; the launch traced here: 423 us
  waiting for transfers between devices  191 us (45%)
  blocking collectives  88.1 us (21%)
  matrix products  72.1 us (17%)
  local copies, waits for them, and re-layouts  32.8 us (8%)
  starting transfers between devices  24.5 us (6%)
  between operations  13.9 us (3%)
    psum x1, blocking collectives, local(): bias_grad = lax.psum(jnp.sum(bias_parts, axis=0), 'row')  88.1 us
    all_gather x1, waiting for transfers between devices, local(): widened = lax.all_gather(layer_input, 'col', axis=1, tiled=True)  52.5 us
    all_gather x1, waiting for transfers between devices, local(): lax.all_gather(query_grad, 'row', axis=0, tiled=True)  47.3 us
    all_gather x1, waiting for transfers between devices, local(): lax.all_gather(value_grad, 'row', axis=0, tiled=True)  45.1 us
    all_gather x1, waiting for transfers between devices, local(): lax.all_gather(key_grad, 'row', axis=0, tiled=True)  45.1 us
    dot_general x3, matrix products, local(): lax.dot_general(spread, member, (((0,), (0,)), ((), ())), preferred_eleme...  29.4 us
    unnamed x26, local copies, waits for them, and re-layouts  17.2 us
    dot_general x1, matrix products, local(): lax.dot_general(flat_grads[2], w_value, contract, preferred_element_type=...  12 us
  transfers between devices with their start and end apart: 8, of which 5 were waited for; matrix products, arithmetic and copies ran while one was open for 20% of the time, Pallas kernels for 0%

commit v1 on v0

v1 whole, which is shorter than its diff:
```python
import functools

import jax
import jax.numpy as jnp
from jax import lax
from jax.experimental import pallas as pl
from jax.experimental.pallas import tpu as pltpu
from jax.sharding import PartitionSpec as P

BF = jnp.bfloat16
F32 = jnp.float32
MESH_ID = pl.DeviceIdType.MESH

ROWS, COLS = 16, 8
TOK, WIDTH, DEPTH = 256, 1024, 512
HEADS, HD = 8, 128
HALF = TOK // 2
PAIRS = 8
NT = (((1,), (1,)), ((), ()))
TN = (((0,), (0,)), ((), ()))
NN = (((1,), (0,)), ((), ()))

Z_FIRST = (0, 1)
ALL = (0, 1, 2, 3, 4, 5)
X_FIRST = tuple(ch for ch in ALL if ch not in Z_FIRST)


def dot(a, b, dims):
    return lax.dot_general(a, b, dims, preferred_element_type=F32)


def row_of(z, xl, core):
    return (z * 2 + xl) * 2 + core


def col_of(y, xh):
    return y * 2 + xh


def kernel(
    x_ref, g_ref, q_ref, k_ref, v_ref, mask_ref, kb_ref, wq_ref, wk_ref, wv_ref,
    layer_out, dwq_out, dwk_out, dwv_out, bias_out,
    grads, xt, xt_send, dw, wt, mcol,
    part, got1, send2, got2, own2, last, landed, bias_send, bias_got,
    g_recv, g_send, xs_send, xs_recv, xt_recv, xt_ssem,
    r1_send, r1_recv, r2_send, r2_recv, f_send, f_recv, b_send, b_recv,
):
    row = lax.axis_index("row")
    col = lax.axis_index("col")
    z = lax.div(row, 4)
    xl = lax.rem(lax.div(row, 2), 2)
    core = lax.rem(row, 2)
    y = lax.div(col, 2)
    xh = lax.rem(col, 2)
    up, down = lax.rem(z + 1, 4), lax.rem(z + 3, 4)
    scale = 1.0 / (HD ** 0.5)
    sends = []

    def remote(src, dst, ssem, rsem, to):
        return pltpu.make_async_remote_copy(
            src_ref=src, dst_ref=dst, send_sem=ssem, recv_sem=rsem, device_id=to, device_id_type=MESH_ID
        )

    def chunk(r, ch):
        return grads.at[r, ch // 2, ch % 2]

    def g_copy(r, ch, to_row, slot):
        return remote(chunk(r, ch), chunk(r, ch), g_send.at[slot], g_recv.at[r, ch], (to_row, col))

    def g_put(r, ch, to_row):
        slot = len(sends)
        copy = g_copy(r, ch, to_row, slot)
        copy.start()
        sends.append((r, ch, to_row, slot))

    def g_wait(r, ch):
        g_copy(r, ch, row_of(z, xl, 1 - core), 0).wait_recv()

    to_up = row_of(up, xl, core)
    to_down = row_of(down, xl, core)
    to_x = row_of(z, 1 - xl, core)
    to_sib = row_of(z, xl, 1 - core)

    sources = {
        (dz, dx): row_of(lax.rem(z + dz, 4), lax.rem(xl + dx, 2), core) for dz in range(4) for dx in range(2)
    }

    def src(dz, dx):
        return sources[dz, dx]

    def from_z(dx, ch):
        low, high = src(3, dx), src(1, dx)
        for r, way in ((low, to_up if ch % 2 == 0 else None), (high, to_down if ch % 2 == 1 else None)):
            g_wait(r, ch)
            if way is not None:
                g_put(r, ch, way)
            if dx == 0 and ch in Z_FIRST:
                g_put(r, ch, to_x)
            g_put(r, ch, to_sib)

    def from_x(ch):
        r = src(0, 1)
        g_wait(r, ch)
        g_put(r, ch, to_up)
        g_put(r, ch, to_down)
        g_put(r, ch, to_sib)

    def far_x(dz, ch):
        r = src(dz, 1)
        g_wait(r, ch)
        g_put(r, ch, to_sib)

    def far_z(dx, ch):
        r = src(2, dx)
        g_wait(r, ch)
        if dx == 0 and ch in Z_FIRST:
            g_put(r, ch, to_x)
        g_put(r, ch, to_sib)

    x_sends = []

    def x_half(s, hs):
        return xt.at[s, pl.ds(hs * 2, 2)]

    def x_copy(s, hs, to_col, slot):
        return remote(x_half(s, hs), x_half(s, hs), xt_ssem.at[slot], xt_recv.at[s, hs], (row, to_col))

    def x_put(s, hs, to_col):
        slot = len(x_sends)
        x_copy(s, hs, to_col, slot).start()
        x_sends.append((s, hs, to_col, slot))

    def x_wait(s, hs):
        x_copy(s, hs, col_of(y, 1 - xh), 0).wait_recv()

    y_up, y_down = lax.rem(y + 1, 4), lax.rem(y + 3, 4)

    def x_first(h, k):
        to_row = row_of(y, xh, k)
        to_col = col_of(2 * core + h, xl)
        here = (to_row == row) & (to_col == col)

        def away():
            return remote(
                xt_send.at[h, k], xt.at[to_col, z], xs_send.at[h, k], xs_recv.at[z], (to_row, to_col)
            )

        def near():
            return pltpu.make_async_copy(xt_send.at[h, k], xt.at[to_col, z], xs_recv.at[z])

        return here, away, near

    def x_first_start(h, k):
        here, away, near = x_first(h, k)

        @pl.when(here)
        def _():
            near().start()

        @pl.when(jnp.logical_not(here))
        def _():
            away().start()

    def x_first_sent(h, k):
        here, away, _ = x_first(h, k)

        @pl.when(jnp.logical_not(here))
        def _():
            away().wait_send()

    def x_own():
        for zs in range(4):
            piece = xt.at[col, zs]
            pltpu.make_async_copy(piece, piece, xs_recv.at[zs]).wait()
        for hs in range(2):
            x_put(col, hs, col_of(y, 1 - xh))
            x_put(col, hs, col_of(y_up, xh))
            x_put(col, hs, col_of(y_down, xh))

    def x_across():
        other = col_of(y, 1 - xh)
        for hs in range(2):
            x_wait(other, hs)
            x_put(other, hs, col_of(y_up, xh))
            x_put(other, hs, col_of(y_down, xh))

    def x_near(xhs):
        for hs in range(2):
            low, high = col_of(y_down, xhs), col_of(y_up, xhs)
            x_wait(low, hs)
            if hs == 0:
                x_put(low, hs, col_of(y_up, xh))
            x_wait(high, hs)
            if hs == 1:
                x_put(high, hs, col_of(y_down, xh))

    def x_far(xhs):
        for hs in range(2):
            x_wait(col_of(lax.rem(y + 2, 4), xhs), hs)

    bias_to = (
        to_sib,
        to_x,
        row_of(z + 1 - 2 * lax.rem(z, 2), xl, core),
        row_of(lax.rem(z + 2, 4), xl, core),
    )

    def bias_copy(level):
        return remote(
            bias_send.at[level], bias_got.at[level], b_send.at[level], b_recv.at[level], (bias_to[level], col)
        )

    def bias_step(level):
        bias_copy(level).wait_recv()
        total = bias_send[level] + bias_got[level]
        if level < 3:
            bias_send[level + 1] = total
            bias_copy(level + 1).start()
        else:
            bias_out[...] = total[:1, :HEADS]

    for h in range(2):
        for k in range(2):
            xt_send[h, k] = x_ref[h * HALF:(h + 1) * HALF, k * DEPTH:(k + 1) * DEPTH].T
            x_first_start(h, k)
    mcol[...] = jnp.broadcast_to(mask_ref[...].astype(F32), (128, TOK)).T
    bias_send[0] = jnp.zeros((8, 128), F32)

    def head(h, carry):
        at = pl.ds(pl.multiple_of(h * HD, HD), HD)
        q, k, v, g = q_ref[:, at], k_ref[:, at], v_ref[:, at], g_ref[:, at]
        flag = jnp.concatenate([mcol[...], mcol[...]], axis=1)
        scores = dot(k, q, NT) * scale + flag * kb_ref[h]
        terms = jnp.exp(scores - jnp.max(scores, axis=0, keepdims=True))
        probs = terms * (1.0 / jnp.sum(terms, axis=0, keepdims=True))
        low = probs.astype(BF)
        grad_probs = dot(v, g, NT)
        delta = jnp.sum(low.astype(F32) * grad_probs, axis=0, keepdims=True)
        grad_scores = probs * (grad_probs - delta)
        grad_low = grad_scores.astype(BF)
        part_sum = jnp.sum(jnp.sum(grad_scores * flag, axis=0, keepdims=True), axis=1, keepdims=True)
        lane = lax.broadcasted_iota(jnp.int32, (8, 128), 1)
        bias_send[0] = bias_send[0] + jnp.where(lane == h, jnp.broadcast_to(part_sum, (8, 128)), 0.0)
        query_grad = (dot(grad_low, k, TN) * scale).astype(BF)
        key_grad = (dot(grad_low, q, NN) * scale).astype(BF)
        value_grad = dot(low, g, NN).astype(BF)
        for a, member in enumerate((query_grad, key_grad, value_grad)):
            for half in range(2):
                grads[row, a, half, :, at] = member[half * HALF:(half + 1) * HALF]
        return carry

    lax.fori_loop(0, HEADS, head, 0)

    for ch in X_FIRST:
        g_put(row, ch, to_x)
    for ch in ALL:
        g_put(row, ch, to_up)
        g_put(row, ch, to_down)
    for ch in Z_FIRST:
        g_put(row, ch, to_x)
    for ch in ALL:
        g_put(row, ch, to_sib)
    bias_copy(0).start()
    x_own()

    for a, w_ref in enumerate((wq_ref, wk_ref, wv_ref)):
        wt[a] = w_ref[...].T
    def clear(t, carry):
        dw[lax.div(t, 4), :, pl.ds(pl.multiple_of(lax.rem(t, 4) * 256, 256), 256)] = jnp.zeros((DEPTH, 256), F32)
        return carry

    lax.fori_loop(0, 12, clear, 0)

    from_x(2)
    from_z(0, 0)
    bias_step(0)
    x_across()
    from_x(3)
    from_z(0, 1)
    bias_step(1)
    x_near(xh)
    from_x(4)
    from_z(0, 2)
    from_x(5)
    from_z(0, 3)
    bias_step(2)
    x_near(1 - xh)
    from_z(0, 4)
    far_x(0, 0)
    from_z(0, 5)
    far_x(0, 1)
    bias_step(3)
    x_far(xh)
    x_far(1 - xh)

    def both_x(ch):
        far_x(1, ch)
        far_x(3, ch)

    events = {
        (0, 1): [lambda: far_z(0, 0)],
        (1, 0): [lambda: both_x(0)],
        (1, 1): [lambda: far_z(0, 1), lambda: from_z(1, 2)],
        (2, 0): [lambda: both_x(1)],
        (2, 1): [lambda: from_z(1, 3)],
        (3, 0): [lambda: far_z(0, 2), lambda: far_z(0, 3)],
        (3, 1): [lambda: from_z(1, 4)],
        (4, 0): [lambda: from_z(1, 5)],
        (4, 1): [lambda: far_x(2, 0)],
        (5, 0): [lambda: far_x(2, 1)],
        (6, 0): [lambda: far_z(0, 4), lambda: far_z(0, 5)],
        (7, 0): [lambda: far_z(1, 2), lambda: far_z(1, 3), lambda: far_z(1, 4), lambda: far_z(1, 5)],
    }

    def place(j):
        late = lax.div(j, 6)
        k = lax.rem(j, 3)
        dx = (1 - late) * lax.div(j, 3) + late * (j - 6)
        dz = (1 - late) * (k + lax.div(k, 2)) + late * 2
        return lax.rem(z + dz, 4), lax.rem(xl + dx, 2)

    def copy1(j, d):
        there = lax.rem(y + d, 4)
        return remote(
            part.at[j, there], got1.at[j, d - 1], r1_send.at[j, d - 1], r1_recv.at[j, d - 1],
            (row, col_of(there, xh)),
        )

    def copy2(j):
        return remote(send2.at[j], got2.at[j], r2_send.at[j], r2_recv.at[j], (row, col_of(y, 1 - xh)))

    def copy3(j, cs):
        zs, xs = place(j)
        to_row, to_col = row_of(zs, xs, cs), lax.div(row, 2)
        here = (to_row == row) & (to_col == col)
        k = lax.rem(row, 2)

        def away():
            return remote(
                last.at[j, cs], landed.at[k, col], f_send.at[j, cs], f_recv.at[k, col], (to_row, to_col)
            )

        def near():
            return pltpu.make_async_copy(last.at[j, cs], landed.at[k, col], f_recv.at[k, col])

        return here, away, near

    mine = pl.ds(pl.multiple_of(xh * 32, 32), 32)
    theirs = pl.ds(pl.multiple_of((1 - xh) * 32, 32), 32)

    def sum1(j):
        for d in (1, 2, 3):
            copy1(j, d).wait_recv()

        def over(at):
            total = part[j, y, :, at, :].astype(F32)
            for d in range(3):
                total = total + got1[j, d, :, at, :].astype(F32)
            return total

        send2[j] = over(theirs).astype(BF)
        copy2(j).start()
        own2[j] = over(mine)

    def sum2(j):
        copy2(j).wait_recv()
        last[j] = (own2[j] + got2[j].astype(F32)).astype(BF)
        for cs in range(2):
            here, away, near = copy3(j, cs)

            @pl.when(here)
            def _():
                near().start()

            @pl.when(jnp.logical_not(here))
            def _():
                away().start()

    def step(j, carry):
        for (at, half), todo in events.items():
            if half == 0:
                @pl.when(j == at)
                def _():
                    for one in todo:
                        one()
        zs, xs = place(j)
        for ch in ALL:
            g_wait(row_of(zs, xs, 1 - core), ch)
        for cs in range(2):
            r = row_of(zs, xs, cs)
            for n in range(2):
                total = None
                for a in range(3):
                    term = dot(
                        grads[r, a].reshape(TOK, WIDTH), wt[a, :, n * 256:(n + 1) * 256], NN
                    )
                    total = term if total is None else total + term
                part[j, :, cs, :, n * 256:(n + 1) * 256] = total.astype(BF).reshape(4, 64, 256)
        for d in (2, 1, 3):
            copy1(j, d).start()

        @pl.when(j >= 2)
        def _():
            sum2(j - 2)

        @pl.when(j >= 1)
        def _():
            sum1(j - 1)

        for (at, half), todo in events.items():
            if half == 1:
                @pl.when(j == at)
                def _():
                    for one in todo:
                        one()

        left = jnp.concatenate([xt[y4 * 2 + xs, zs] for y4 in range(4)], axis=1)

        for a in range(3):
            for n in range(4):
                cols = slice(n * 256, (n + 1) * 256)
                r0, r1 = row_of(zs, xs, 0), row_of(zs, xs, 1)
                right = jnp.concatenate(
                    [grads[r0, a, :, :, cols].reshape(TOK, 256), grads[r1, a, :, :, cols].reshape(TOK, 256)], axis=0
                )
                dw[a, :, cols] = dw[a, :, cols] + dot(left, right, NN)
        return carry

    lax.fori_loop(0, PAIRS, step, 0)

    sum2(PAIRS - 2)
    sum1(PAIRS - 1)
    for a, out in enumerate((dwq_out, dwk_out, dwv_out)):
        for n in range(4):
            out[:, n * 256:(n + 1) * 256] = dw[a, :, n * 256:(n + 1) * 256].astype(BF)
    sum2(PAIRS - 1)

    for r, ch, to_row, slot in sends:
        g_copy(r, ch, to_row, slot).wait_send()
    for s, hs, to_col, slot in x_sends:
        x_copy(s, hs, to_col, slot).wait_send()
    for h in range(2):
        for k in range(2):
            x_first_sent(h, k)
    for level in range(4):
        bias_copy(level).wait_send()

    def sent(j, carry):
        for d in (1, 2, 3):
            copy1(j, d).wait_send()
        copy2(j).wait_send()
        for cs in range(2):
            here, away, _ = copy3(j, cs)

            @pl.when(jnp.logical_not(here))
            def _():
                away().wait_send()
        return carry

    lax.fori_loop(0, PAIRS, sent, 0)
    for k in range(2):
        for s in range(COLS):
            piece = landed.at[k, s]
            pltpu.make_async_copy(piece, piece, f_recv.at[k, s]).wait()
            layer_out[s * 32:(s + 1) * 32, k * DEPTH:(k + 1) * DEPTH] = landed[k, s]


def local(layer_input, attn_grad, queries, keys, values, masked, key_bias, w_query, w_key, w_value):
    vmem = pl.BlockSpec(memory_space=pltpu.VMEM)
    smem = pl.BlockSpec(memory_space=pltpu.SMEM)
    dma = pltpu.SemaphoreType.DMA
    outs = pl.pallas_call(
        kernel,
        out_shape=(
            jax.ShapeDtypeStruct((TOK, WIDTH), BF),
            jax.ShapeDtypeStruct((DEPTH, WIDTH), BF),
            jax.ShapeDtypeStruct((DEPTH, WIDTH), BF),
            jax.ShapeDtypeStruct((DEPTH, WIDTH), BF),
            jax.ShapeDtypeStruct((1, HEADS), F32),
        ),
        in_specs=[vmem] * 6 + [smem] + [vmem] * 3,
        out_specs=(vmem,) * 5,
        scratch_shapes=[
            pltpu.VMEM((ROWS, 3, 2, HALF, WIDTH), BF),
            pltpu.VMEM((COLS, 4, DEPTH, HALF), BF),
            pltpu.VMEM((2, 2, DEPTH, HALF), BF),
            pltpu.VMEM((3, DEPTH, WIDTH), F32),
            pltpu.VMEM((3, WIDTH, DEPTH), BF),
            pltpu.VMEM((TOK, 128), F32),
            pltpu.VMEM((PAIRS, 4, 2, 64, DEPTH), BF),
            pltpu.VMEM((PAIRS, 3, 2, 64, DEPTH), BF),
            pltpu.VMEM((PAIRS, 2, 32, DEPTH), BF),
            pltpu.VMEM((PAIRS, 2, 32, DEPTH), BF),
            pltpu.VMEM((PAIRS, 2, 32, DEPTH), F32),
            pltpu.VMEM((PAIRS, 2, 32, DEPTH), BF),
            pltpu.VMEM((2, COLS, 32, DEPTH), BF),
            pltpu.VMEM((4, 8, 128), F32),
            pltpu.VMEM((4, 8, 128), F32),
            dma((ROWS, 6)),
            dma((96,)),
            dma((2, 2)),
            dma((4,)),
            dma((COLS, 2)),
            dma((16,)),
            dma((PAIRS, 3)),
            dma((PAIRS, 3)),
            dma((PAIRS,)),
            dma((PAIRS,)),
            dma((PAIRS, 2)),
            dma((2, COLS)),
            dma((4,)),
            dma((4,)),
        ],
        compiler_params=pltpu.CompilerParams(has_side_effects=True, vmem_limit_bytes=62 * 2**20),
    )(
        layer_input, attn_grad, queries[0], keys[0], values[0], masked, key_bias, w_query, w_key, w_value
    )
    return outs[0], outs[1], outs[2], outs[3], outs[4].reshape(HEADS)


def solution(mesh):
    in_specs = (
        P("row", "col"),
        P("row", "col"),
        P("row", None, "col"),
        P("row", None, "col"),
        P("row", None, "col"),
        P("row", None),
        P("col"),
        P("row", "col"),
        P("row", "col"),
        P("row", "col"),
    )
    out_specs = (P("row", "col"), P("row", "col"), P("row", "col"), P("row", "col"), P("col"))
    return jax.shard_map(local, mesh=mesh, in_specs=in_specs, out_specs=out_specs, check_vma=False)
```

time: 426 us -> 197 us (0.46)
  waiting for transfers between devices: 191 us -> 0 us
  Pallas kernels: 0 us -> 189 us
  blocking collectives: 88.1 us -> 0 us
  matrix products: 72.1 us -> 0 us
  local copies, waits for them, and re-layouts: 32.8 us -> 6.65 us
  starting transfers between devices: 24.5 us -> 0 us
  between operations: 13.9 us -> 0.66 us
    all_gather x4 -> x0, waiting for transfers between devices: 190 us -> none  [the longest x1 52.5 us: local(): widened = lax.all_gather(layer_input, 'col', axis=1, tiled=True)]
    pallas_call x0 -> x1, Pallas kernels: none -> 189 us  [local(): pl.pallas_call(kernel, out_shape=(jax.ShapeDtypeStruct((TOK, WIDTH), BF),...]
    psum x1 -> x0, blocking collectives: 88.1 us -> none  [local(): bias_grad = lax.psum(jnp.sum(bias_parts, axis=0), 'row')]
    dot_general x11 -> x0, matrix products: 69.9 us -> none  [the longest x3 29.4 us: local(): lax.dot_general(spread, member, (((0,), (0,)), ((), ())), preferred_eleme...]
    all_to_all x3 -> x0, starting transfers between devices: 24.1 us -> none  [the longest x1 10.7 us: local(): lax.all_to_all(sectioned, 'row', split_axis=0, concat_axis=2, tiled=True)]
    unnamed x26 -> x13, local copies, waits for them, and re-layouts: 17.2 us -> 6.65 us
    all_to_all x2 -> x0, local copies, waits for them, and re-layouts: 6.48 us -> none  [the longest x1 6.44 us: local(): lax.all_to_all(widened, 'row', split_axis=1, concat_axis=0, tiled=True)]
    reshape x4 -> x0, local copies, waits for them, and re-layouts: 5.06 us -> none  [the longest x1 1.43 us: attend_back(): query_h = query_c.reshape(length, heads_local, head_dim)]
  transfers between devices with their start and end apart: 8 -> 0, of which waited for: 5 -> 0; matrix products, arithmetic and copies ran while one was open for 20% -> 0% of each run, Pallas kernels for 0% -> 0%
where the time goes in v1:
time: 197 us
  Pallas kernels  189 us (96%)
  local copies, waits for them, and re-layouts  6.65 us (3%)
    pallas_call x1, Pallas kernels, local(): pl.pallas_call(kernel, out_shape=(jax.ShapeDtypeStruct((TOK, WIDTH), BF),...  189 us
    unnamed x13, local copies, waits for them, and re-layouts  6.65 us

profile of v1, /device:TPU:109, one launch (start us, length us, event | category | flops | bytes accessed | tf_op | source)
XLA Modules:
  0.0 196.7 jit_solution(7219739256980850122)
XLA Ops:
  0.6 189.4 %shard_map.137 = (bf16[256,1024]{1,0:T(8,128)(2,1)}, bf16[512,1024]{1,0:T(8,128)(2,1)}, bf16[512,1024]{1,0:T(8,128)(2,1)}, bf16[512,1024]{1,0:T(8,128)(2,1)}, f32[1,8]{1,0:T(1,128)}) custom-call(bf16[256,1024]{1,0:T(8,128)(2,1)} %x_ref.1, bf16[256,1024]{1,0:T(8,128)(2,1)} %g_ref.1, bf16[256,1024]{1,0:T(8,128)(2,1)} %bitcast.4, bf16[256,1024]{1,0:T(8,128)(2,1)} %bitcast.5, ...), custom_call_target="tpu_custom_call" | custom-call | tf_op jit(solution)/shard_map/pallas_call | solution.py:472
  190.1 0.0 copy-start.2
  190.1 2.0 copy.20
  192.0 0.0 copy-done.2
  192.0 0.0 copy-start.1
  192.0 1.0 copy.21
  193.0 0.6 copy-done.1
  193.6 0.0 copy-start
  193.6 1.0 copy.22
  194.6 0.6 copy-done
  195.2 0.0 copy-start.3
  195.3 1.0 copy.23
  196.2 0.0 copy-done.3
  196.2 0.5 copy.24
Async XLA Ops:
  190.1 2.0 %copy-start.2 = (bf16[512,1024]{1,0:T(8,128)(2,1)S(1)}, bf16[512,1024]{1,0:T(8,128)(2,1)}, u32[]{:S(2)}) copy-start(bf16[512,1024]{1,0:T(8,128)(2,1)} %get-tuple-element.21) | copy-start | bytes 3145732
  192.0 1.6 copy-start.1
  193.6 1.6 copy-start
  195.2 1.0 copy-start.3

commit v2 on v1

--- a/solution.py
+++ b/solution.py
@@ -15,14 +15,76 @@
 TOK, WIDTH, DEPTH = 256, 1024, 512
 HEADS, HD = 8, 128
 HALF = TOK // 2
+SPLIT = WIDTH // 2
 PAIRS = 8
 NT = (((1,), (1,)), ((), ()))
 TN = (((0,), (0,)), ((), ()))
 NN = (((1,), (0,)), ((), ()))
 
 Z_FIRST = (0, 1)
-ALL = (0, 1, 2, 3, 4, 5)
+ALL = (0, 2, 4, 1, 3, 5)
 X_FIRST = tuple(ch for ch in ALL if ch not in Z_FIRST)
+
+BEFORE = (
+    ("attend", 0), ("start",), ("own", "d", 4), ("own", "d", 2), ("attend", 1), ("own", "u", 4),
+    ("own", "u", 5), ("own", "x", 3), ("own", "d", 0), ("own", "u", 0), ("own", "d", 1), ("own", "u", 2),
+    ("own", "x", 5), ("own", "u", 1), ("x_arrived",), ("x_over",), ("x_round",), ("own", "s", 4),
+    ("own", "d", 3), ("own", "u", 3), ("own", "s", 3), ("from_z", 0, 4), ("own", "x", 2), ("x_near", 0),
+    ("own", "x", 4), ("x_across", 0), ("own", "x", 0), ("from_z", 0, 2), ("own", "d", 5), ("prepare",),
+    ("own", "x", 1), ("x_across", 1), ("from_x", 2), ("from_x", 5), ("own", "s", 2), ("from_z", 0, 0),
+    ("from_z", 0, 1), ("from_z", 0, 3), ("x_near", 1), ("hop", 0, 0), ("from_z", 0, 5), ("own", "s", 5),
+    ("hop", 0, 3), ("x_far", 0), ("own", "s", 1), ("from_x", 3),
+)
+STEPS = (
+    ("D", 2, (
+    )),
+    ("D", 1, (
+        ("from_x", 4), ("own", "s", 0), ("hop", 0, 4),
+    )),
+    ("W", 2, (
+        ("x_far", 1), ("far_x", 0, 0), ("far_x", 0, 1), ("hop", 0, 5), ("bias", 0),
+    )),
+    ("D", 3, (
+    )),
+    ("D", 0, (
+        ("hop", 0, 2), ("hop", 0, 1), ("far_x", 3, 0),
+    )),
+    ("W", 3, (
+        ("from_z", 1, 5),
+    )),
+    ("W", 0, (
+        ("from_z", 1, 2), ("bias", 1),
+    )),
+    ("W", 1, (
+    )),
+    ("D", 5, (
+        ("sum1", 2), ("far_z", 0, 3), ("from_z", 1, 4), ("far_z", 0, 0), ("far_x", 3, 1), ("from_z", 1, 3),
+        ("sum1", 3), ("far_x", 1, 0), ("far_z", 0, 5), ("far_x", 1, 1),
+    )),
+    ("W", 5, (
+    )),
+    ("D", 4, (
+        ("bias", 2),
+    )),
+    ("W", 4, (
+        ("sum2", 2), ("far_x", 2, 0), ("far_z", 0, 4), ("far_z", 0, 2), ("far_z", 0, 1),
+    )),
+    ("D", 6, (
+        ("far_z", 1, 5), ("far_z", 1, 2), ("sum1", 0),
+    )),
+    ("D", 7, (
+        ("sum2", 3), ("far_x", 2, 1), ("sum1", 1), ("sum1", 5), ("sum2", 0), ("far_z", 1, 4), ("far_z", 1, 3),
+        ("sum1", 4), ("sum2", 1),
+    )),
+    ("W", 7, (
+        ("sum1", 6), ("bias", 3),
+    )),
+    ("W", 6, (
+    )),
+)
+AFTER = (
+    ("sum2", 5), ("sum2", 4), ("sum2", 6), ("sum1", 7), ("sum2", 7),
+)
 
 
 def dot(a, b, dims):
@@ -88,12 +150,20 @@
     def src(dz, dx):
         return sources[dz, dx]
 
+    def hop(dx, ch):
+        if ch % 2 == 0:
+            g_put(src(3, dx), ch, to_up)
+        else:
+            g_put(src(1, dx), ch, to_down)
+
     def from_z(dx, ch):
-        low, high = src(3, dx), src(1, dx)
-        for r, way in ((low, to_up if ch % 2 == 0 else None), (high, to_down if ch % 2 == 1 else None)):
-            g_wait(r, ch)
-            if way is not None:
-                g_put(r, ch, way)
+        if dx == 1:
+            g_wait(src(1 if ch % 2 else 3, 1), ch)
+            hop(1, ch)
+            g_wait(src(3 if ch % 2 else 1, 1), ch)
+        for r in (src(3, dx), src(1, dx)):
+            if dx == 0:
+                g_wait(r, ch)
             if dx == 0 and ch in Z_FIRST:
                 g_put(r, ch, to_x)
             g_put(r, ch, to_sib)
@@ -168,23 +238,28 @@
         def _():
             away().wait_send()
 
-    def x_own():
+    def x_arrived():
         for zs in range(4):
             piece = xt.at[col, zs]
             pltpu.make_async_copy(piece, piece, xs_recv.at[zs]).wait()
+
+    def x_over():
         for hs in range(2):
             x_put(col, hs, col_of(y, 1 - xh))
+
+    def x_round():
+        for hs in range(2):
             x_put(col, hs, col_of(y_up, xh))
             x_put(col, hs, col_of(y_down, xh))
 
-    def x_across():
+    def x_across(hs):
         other = col_of(y, 1 - xh)
-        for hs in range(2):
-            x_wait(other, hs)
-            x_put(other, hs, col_of(y_up, xh))
-            x_put(other, hs, col_of(y_down, xh))
-
-    def x_near(xhs):
+        x_wait(other, hs)
+        x_put(other, hs, col_of(y_up, xh))
+        x_put(other, hs, col_of(y_down, xh))
+
+    def x_near(other):
+        xhs = 1 - xh if other else xh
         for hs in range(2):
             low, high = col_of(y_down, xhs), col_of(y_up, xhs)
             x_wait(low, hs)
@@ -194,7 +269,8 @@
             if hs == 1:
                 x_put(high, hs, col_of(y_down, xh))
 
-    def x_far(xhs):
+    def x_far(other):
+        xhs = 1 - xh if other else xh
         for hs in range(2):
             x_wait(col_of(lax.rem(y + 2, 4), xhs), hs)
 
@@ -219,15 +295,31 @@
         else:
             bias_out[...] = total[:1, :HEADS]
 
+    ready = pltpu.get_barrier_semaphore()
+    for to in (
+        (to_up, col), (to_down, col), (row_of(lax.rem(z + 2, 4), xl, core), col), (to_x, col), (to_sib, col),
+        (row, col_of(y_up, xh)), (row, col_of(y_down, xh)), (row, col_of(lax.rem(y + 2, 4), xh)),
+        (row, col_of(y, 1 - xh)),
+    ):
+        pl.semaphore_signal(ready, inc=1, device_id=to, device_id_type=MESH_ID)
+    for zs in range(4):
+        from_row, from_col = row_of(zs, xh, lax.div(y, 2)), col_of(z, xl)
+        itself = (from_row == row) & (from_col == col)
+
+        @pl.when(jnp.logical_not(itself))
+        def _():
+            pl.semaphore_signal(ready, inc=1, device_id=(from_row, from_col), device_id_type=MESH_ID)
+
     for h in range(2):
         for k in range(2):
             xt_send[h, k] = x_ref[h * HALF:(h + 1) * HALF, k * DEPTH:(k + 1) * DEPTH].T
-            x_first_start(h, k)
     mcol[...] = jnp.broadcast_to(mask_ref[...].astype(F32), (128, TOK)).T
     bias_send[0] = jnp.zeros((8, 128), F32)
 
-    def head(h, carry):
+    def head(half, n, carry):
+        h = half * 4 + n
         at = pl.ds(pl.multiple_of(h * HD, HD), HD)
+        to = pl.ds(pl.multiple_of(n * HD, HD), HD)
         q, k, v, g = q_ref[:, at], k_ref[:, at], v_ref[:, at], g_ref[:, at]
         flag = jnp.concatenate([mcol[...], mcol[...]], axis=1)
         scores = dot(k, q, NT) * scale + flag * kb_ref[h]
@@ -245,72 +337,8 @@
         key_grad = (dot(grad_low, q, NN) * scale).astype(BF)
         value_grad = dot(low, g, NN).astype(BF)
         for a, member in enumerate((query_grad, key_grad, value_grad)):
-            for half in range(2):
-                grads[row, a, half, :, at] = member[half * HALF:(half + 1) * HALF]
+            grads[row, a, half, :, to] = member
         return carry
-
-    lax.fori_loop(0, HEADS, head, 0)
-
-    for ch in X_FIRST:
-        g_put(row, ch, to_x)
-    for ch in ALL:
-        g_put(row, ch, to_up)
-        g_put(row, ch, to_down)
-    for ch in Z_FIRST:
-        g_put(row, ch, to_x)
-    for ch in ALL:
-        g_put(row, ch, to_sib)
-    bias_copy(0).start()
-    x_own()
-
-    for a, w_ref in enumerate((wq_ref, wk_ref, wv_ref)):
-        wt[a] = w_ref[...].T
-    def clear(t, carry):
-        dw[lax.div(t, 4), :, pl.ds(pl.multiple_of(lax.rem(t, 4) * 256, 256), 256)] = jnp.zeros((DEPTH, 256), F32)
-        return carry
-
-    lax.fori_loop(0, 12, clear, 0)
-
-    from_x(2)
-    from_z(0, 0)
-    bias_step(0)
-    x_across()
-    from_x(3)
-    from_z(0, 1)
-    bias_step(1)
-    x_near(xh)
-    from_x(4)
-    from_z(0, 2)
-    from_x(5)
-    from_z(0, 3)
-    bias_step(2)
-    x_near(1 - xh)
-    from_z(0, 4)
-    far_x(0, 0)
-    from_z(0, 5)
-    far_x(0, 1)
-    bias_step(3)
-    x_far(xh)
-    x_far(1 - xh)
-
-    def both_x(ch):
-        far_x(1, ch)
-        far_x(3, ch)
-
-    events = {
-        (0, 1): [lambda: far_z(0, 0)],
-        (1, 0): [lambda: both_x(0)],
-        (1, 1): [lambda: far_z(0, 1), lambda: from_z(1, 2)],
-        (2, 0): [lambda: both_x(1)],
-        (2, 1): [lambda: from_z(1, 3)],
-        (3, 0): [lambda: far_z(0, 2), lambda: far_z(0, 3)],
-        (3, 1): [lambda: from_z(1, 4)],
-        (4, 0): [lambda: from_z(1, 5)],
-        (4, 1): [lambda: far_x(2, 0)],
-        (5, 0): [lambda: far_x(2, 1)],
-        (6, 0): [lambda: far_z(0, 4), lambda: far_z(0, 5)],
-        (7, 0): [lambda: far_z(1, 2), lambda: far_z(1, 3), lambda: far_z(1, 4), lambda: far_z(1, 5)],
-    }
 
     def place(j):
         late = lax.div(j, 6)
@@ -376,64 +404,92 @@
             def _():
                 away().start()
 
-    def step(j, carry):
-        for (at, half), todo in events.items():
-            if half == 0:
-                @pl.when(j == at)
-                def _():
-                    for one in todo:
-                        one()
+    def input_part(j):
         zs, xs = place(j)
         for ch in ALL:
             g_wait(row_of(zs, xs, 1 - core), ch)
         for cs in range(2):
             r = row_of(zs, xs, cs)
+            left = jnp.concatenate([grads[r, a, half] for a in range(3) for half in range(2)], axis=1)
             for n in range(2):
-                total = None
-                for a in range(3):
-                    term = dot(
-                        grads[r, a].reshape(TOK, WIDTH), wt[a, :, n * 256:(n + 1) * 256], NN
-                    )
-                    total = term if total is None else total + term
-                part[j, :, cs, :, n * 256:(n + 1) * 256] = total.astype(BF).reshape(4, 64, 256)
-        for d in (2, 1, 3):
+                cols = slice(n * 256, (n + 1) * 256)
+                part[j, :, cs, :, cols] = dot(left, wt[:, cols], NN).astype(BF).reshape(4, 64, 256)
+        for d in (1, 3, 2):
             copy1(j, d).start()
 
-        @pl.when(j >= 2)
-        def _():
-            sum2(j - 2)
-
-        @pl.when(j >= 1)
-        def _():
-            sum1(j - 1)
-
-        for (at, half), todo in events.items():
-            if half == 1:
-                @pl.when(j == at)
-                def _():
-                    for one in todo:
-                        one()
-
+    def weight_part(j):
+        zs, xs = place(j)
         left = jnp.concatenate([xt[y4 * 2 + xs, zs] for y4 in range(4)], axis=1)
-
+        r0, r1 = row_of(zs, xs, 0), row_of(zs, xs, 1)
         for a in range(3):
             for n in range(4):
                 cols = slice(n * 256, (n + 1) * 256)
-                r0, r1 = row_of(zs, xs, 0), row_of(zs, xs, 1)
-                right = jnp.concatenate(
-                    [grads[r0, a, :, :, cols].reshape(TOK, 256), grads[r1, a, :, :, cols].reshape(TOK, 256)], axis=0
-                )
+                within = slice((n % 2) * 256, (n % 2 + 1) * 256)
+                right = jnp.concatenate([grads[r, a, n // 2, :, within] for r in (r0, r1)], axis=0)
                 dw[a, :, cols] = dw[a, :, cols] + dot(left, right, NN)
+
+    def start_sends():
+        one_is_here = (y == z) & (xh == xl) & (lax.div(y, 2) == core)
+        pl.semaphore_wait(ready, jnp.where(one_is_here, 12, 13))
+        for h in range(2):
+            for k in range(2):
+                x_first_start(h, k)
+
+    def attend(half):
+        lax.fori_loop(0, HEADS // 2, functools.partial(head, half), 0)
+        if half == 1:
+            bias_copy(0).start()
+
+    def prepare():
+        for a, w_ref in enumerate((wq_ref, wk_ref, wv_ref)):
+            wt[a * WIDTH:(a + 1) * WIDTH] = w_ref[...].T
+
+        def clear(t, carry):
+            cols = pl.ds(pl.multiple_of(lax.rem(t, 4) * 256, 256), 256)
+            dw[lax.div(t, 4), :, cols] = jnp.zeros((DEPTH, 256), F32)
+            return carry
+
+        lax.fori_loop(0, 12, clear, 0)
+
+    ways = {"u": to_up, "d": to_down, "x": to_x, "s": to_sib}
+    does = {
+        "attend": attend, "start": start_sends, "own": lambda way, ch: g_put(row, ch, ways[way]),
+        "x_arrived": x_arrived, "x_over": x_over, "x_round": x_round, "x_across": x_across, "x_near": x_near,
+        "x_far": x_far, "hop": hop, "from_z": from_z, "from_x": from_x, "far_x": far_x, "far_z": far_z,
+        "sum1": sum1, "sum2": sum2, "prepare": prepare, "bias": bias_step,
+    }
+
+    def play(todo):
+        for name, *rest in todo:
+            does[name](*rest)
+
+    play(BEFORE)
+
+    def step(k, carry):
+        for at, (_, _, todo) in enumerate(STEPS):
+            if todo:
+                @pl.when(k == at)
+                def _():
+                    play(todo)
+
+        j = sum(jnp.where(k == at, what, 0) for at, (_, what, _) in enumerate(STEPS) if what)
+        weights = sum(jnp.where(k == at, 1, 0) for at, (kind, _, _) in enumerate(STEPS) if kind == "W")
+
+        @pl.when(weights == 0)
+        def _():
+            input_part(j)
+
+        @pl.when(weights == 1)
+        def _():
+            weight_part(j)
+
         return carry
 
-    lax.fori_loop(0, PAIRS, step, 0)
-
-    sum2(PAIRS - 2)
-    sum1(PAIRS - 1)
+    lax.fori_loop(0, len(STEPS), step, 0)
+    play(AFTER)
     for a, out in enumerate((dwq_out, dwk_out, dwv_out)):
         for n in range(4):
             out[:, n * 256:(n + 1) * 256] = dw[a, :, n * 256:(n + 1) * 256].astype(BF)
-    sum2(PAIRS - 1)
 
     for r, ch, to_row, slot in sends:
         g_copy(r, ch, to_row, slot).wait_send()
@@ -481,11 +537,11 @@
         in_specs=[vmem] * 6 + [smem] + [vmem] * 3,
         out_specs=(vmem,) * 5,
         scratch_shapes=[
-            pltpu.VMEM((ROWS, 3, 2, HALF, WIDTH), BF),
+            pltpu.VMEM((ROWS, 3, 2, TOK, SPLIT), BF),
             pltpu.VMEM((COLS, 4, DEPTH, HALF), BF),
             pltpu.VMEM((2, 2, DEPTH, HALF), BF),
             pltpu.VMEM((3, DEPTH, WIDTH), F32),
-            pltpu.VMEM((3, WIDTH, DEPTH), BF),
+            pltpu.VMEM((3 * WIDTH, DEPTH), BF),
             pltpu.VMEM((TOK, 128), F32),
             pltpu.VMEM((PAIRS, 4, 2, 64, DEPTH), BF),
             pltpu.VMEM((PAIRS, 3, 2, 64, DEPTH), BF),
@@ -511,7 +567,7 @@
             dma((4,)),
             dma((4,)),
         ],
-        compiler_params=pltpu.CompilerParams(has_side_effects=True, vmem_limit_bytes=62 * 2**20),
+        compiler_params=pltpu.CompilerParams(collective_id=0, has_side_effects=True, vmem_limit_bytes=62 * 2**20),
     )(
         layer_input, attn_grad, queries[0], keys[0], values[0], masked, key_bias, w_query, w_key, w_value
     )

time: 197 us -> 159 us (0.81)
  Pallas kernels: 189 us -> 150 us
    pallas_call x1, Pallas kernels: 189 us -> 150 us  [local(): pl.pallas_call(kernel, out_shape=(jax.ShapeDtypeStruct((TOK, WIDTH), BF),...]
where the time goes in v2:
time: 159 us; the launch traced here: 158 us
  Pallas kernels  150 us (94%)
  local copies, waits for them, and re-layouts  6.65 us (4%)
    pallas_call x1, Pallas kernels, local(): pl.pallas_call(kernel, out_shape=(jax.ShapeDtypeStruct((TOK, WIDTH), BF),...  150 us
    unnamed x13, local copies, waits for them, and re-layouts  6.65 us

profile of v2, /device:TPU:109, one launch (start us, length us, event | category | flops | bytes accessed | tf_op | source)
XLA Modules:
  0.0 157.7 jit_solution(7025777160994248809)
XLA Ops:
  0.6 150.4 %shard_map.137 = (bf16[256,1024]{1,0:T(8,128)(2,1)}, bf16[512,1024]{1,0:T(8,128)(2,1)}, bf16[512,1024]{1,0:T(8,128)(2,1)}, bf16[512,1024]{1,0:T(8,128)(2,1)}, f32[1,8]{1,0:T(1,128)}) custom-call(bf16[256,1024]{1,0:T(8,128)(2,1)} %x_ref.1, bf16[256,1024]{1,0:T(8,128)(2,1)} %g_ref.1, bf16[256,1024]{1,0:T(8,128)(2,1)} %bitcast.4, bf16[256,1024]{1,0:T(8,128)(2,1)} %bitcast.5, ...), custom_call_target="tpu_custom_call" | custom-call | tf_op jit(solution)/shard_map/pallas_call | solution.py:528
  151.1 0.0 copy-start.2
  151.1 2.0 %copy.20 = bf16[256,1024]{1,0:T(8,128)(2,1)} copy(bf16[256,1024]{1,0:T(8,128)(2,1)} %get-tuple-element.20) | data formatting | bytes 1048576
  153.0 0.0 copy-done.2
  153.0 0.0 copy-start.1
  153.0 1.0 copy.21
  154.0 0.6 copy-done.1
  154.6 0.0 copy-start
  154.7 1.0 copy.22
  155.6 0.6 copy-done
  156.3 0.0 copy-start.3
  156.3 1.0 copy.23
  157.2 0.0 copy-done.3
  157.2 0.5 copy.24
Async XLA Ops:
  151.1 2.0 %copy-start.2 = (bf16[512,1024]{1,0:T(8,128)(2,1)S(1)}, bf16[512,1024]{1,0:T(8,128)(2,1)}, u32[]{:S(2)}) copy-start(bf16[512,1024]{1,0:T(8,128)(2,1)} %get-tuple-element.21) | copy-start | bytes 3145732
  153.0 1.6 %copy-start.1 = (bf16[512,1024]{1,0:T(8,128)(2,1)S(1)}, bf16[512,1024]{1,0:T(8,128)(2,1)}, u32[]{:S(2)}) copy-start(bf16[512,1024]{1,0:T(8,128)(2,1)} %get-tuple-element.22) | copy-start | bytes 3145732
  154.6 1.6 %copy-start = (bf16[512,1024]{1,0:T(8,128)(2,1)S(1)}, bf16[512,1024]{1,0:T(8,128)(2,1)}, u32[]{:S(2)}) copy-start(bf16[512,1024]{1,0:T(8,128)(2,1)} %get-tuple-element.23) | copy-start | bytes 3145732
  156.3 1.0 copy-start.3
